TPU v7x, 32 devices: a whole 2x2x4 slice. The times are simulated.
32 devices in a mesh: dp: 16 (over z, y, core), mp: 2 (over x).
Axes of the slice: x: 2, y: 2, z: 4, core: 2. Of those that a mesh axis runs over, the one named last changes fastest.
Arguments:
- activations: bfloat16 [2, 16384, 512], P(None, 'dp'), may hold values from -6 to 6
- cotangent: bfloat16 [2, 16384, 512], P(None, 'dp'), may hold values from -6 to 6
- w_qkv: bfloat16 [3, 512, 512], P(None, 'dp', 'mp'), may hold values from -0.25 to 0.25
- w_o: bfloat16 [512, 512], P('mp', 'dp'), may hold values from -0.75 to 0.75
- w_up: bfloat16 [512, 2048], P('dp', 'mp'), may hold values from -0.25 to 0.25
- w_down: bfloat16 [2048, 512], P('mp', 'dp'), may hold values from -0.125 to 0.125
- b_qv: bfloat16 [2, 8, 64], P(None, 'mp', 'dp'), may hold values from -3 to 3
- b_up: bfloat16 [32, 64], P('mp', 'dp'), may hold values from -3 to 3
- out_bias: bfloat16 [2, 512], P(None, 'dp'), may hold values from -3 to 3
- norm_gain: bfloat16 [2, 512], P(None, 'dp'), may hold values from 0.25 to 1.75
- norm_bias: bfloat16 [2, 512], P(None, 'dp'), may hold values from -2 to 2
- chain_ids: int32 [2, 16384], P(None, 'dp'), may hold values from -1 to 1023, as said below
- key_keep: int32 [2, 16384], P(None, 'dp'), may hold values 0 or 1
Outputs:
- output: float32 [2, 16384, 512], P(None, 'dp')
- grad_x: float32 [2, 16384, 512], P(None, 'dp')
- grad_w_qkv: float32 [3, 512, 512], P(None, 'dp', 'mp')
- grad_w_o: float32 [512, 512], P('mp', 'dp')
- grad_w_up: float32 [512, 2048], P('dp', 'mp')
- grad_w_down: float32 [2048, 512], P('mp', 'dp')
- grad_b_qv: float32 [2, 8, 64], P(None, 'mp', 'dp')
- grad_b_up: float32 [32, 64], P('mp', 'dp')
- grad_out_bias: float32 [2, 512], P(None, 'dp')
- grad_norm_gain: float32 [2, 512], P(None, 'dp')
- grad_norm_bias: float32 [2, 512], P(None, 'dp')
Inputs may be any that keep to these rules, and one draw needn't show every extreme that they name: `chain_ids`: in each aligned block of 1024 slots along the last dimension, a live slot carries the index within the block of the first slot of its chain, chains are contiguous runs of live slots, the first slot of every block is live, and padding slots (-1) come after all live slots of their block; how many slots are live differs from block to block.
All inputs are finite; a program needn't handle non-finite values. No bound on the sum of `key_keep` on one device may be relied on, other than what follows from the above.
Results may differ from a plain program's by a relative error of at most 0.018.
Values may be sent and summed in bfloat16 or wider, within the bound.
A program may use at most 192 MiB of HBM per device.

v0:
```python
import math
import jax
import jax.numpy as jnp
from jax import lax
from jax.sharding import PartitionSpec as P

epsilon = 1e-05
masked_value = -1e30


def product(left, right):
    return jnp.dot(left, right, preferred_element_type=jnp.float32)


def normalize(values, scale_row, shift_row):
    row_mean = jnp.mean(values, axis=-1, keepdims=True)
    centred = values - row_mean
    inverse = lax.rsqrt(jnp.mean(centred * centred, axis=-1, keepdims=True) + epsilon)
    scaled = centred * inverse
    return (scaled * scale_row + shift_row, scaled, inverse)


def normalize_back(grad_rows, scaled, inverse, scale_row):
    inner = grad_rows * scale_row
    return inverse * (
        inner
        - jnp.mean(inner, axis=-1, keepdims=True)
        - scaled * jnp.mean(inner * scaled, axis=-1, keepdims=True)
    )


def gelu_slope(values):
    normal_cdf = 0.5 * (1.0 + lax.erf(values * 0.7071067811865476))
    density = jnp.exp(-0.5 * values * values) * 0.3989422804014327
    return normal_cdf + values * density


def permitted(chain_rows, keep_rows):
    slot_count = chain_rows.shape[0]
    same_chain = chain_rows[:, None] == chain_rows[None, :]
    diagonal = lax.broadcasted_iota(jnp.int32, (slot_count, slot_count), 0) == lax.broadcasted_iota(
        jnp.int32, (slot_count, slot_count), 1
    )
    return same_chain & ((keep_rows[None, :] == 1) | diagonal)


def head_scores(query, key_rows, allowed, head_count, head_width):
    query_heads = query.reshape(-1, head_count, head_width)
    key_heads = key_rows.reshape(-1, head_count, head_width)
    scores = jnp.einsum(
        "qhd,khd->hqk", query_heads, key_heads, preferred_element_type=jnp.float32
    ) * (1.0 / math.sqrt(head_width))
    return jnp.where(allowed[None], scores, masked_value)


def forward(rows_in, chain_rows, keep_rows, weights):
    qkv_full, out_full, up_full, down_full, bias_qv, bias_up, bias_out, gain_full, shift_full = (
        weights
    )
    head_count = bias_qv.shape[1]
    head_width = bias_qv.shape[2]
    row_count = rows_in.shape[0]
    bias_qv = bias_qv.astype(jnp.float32)
    bias_out = bias_out.astype(jnp.float32)
    gain_full = gain_full.astype(jnp.float32)
    shift_full = shift_full.astype(jnp.float32)
    allowed = permitted(chain_rows, keep_rows)
    normed_one, scaled_one, inverse_one = normalize(rows_in, gain_full[0], shift_full[0])
    hidden_one = normed_one.astype(jnp.bfloat16)
    query = (product(hidden_one, qkv_full[0]) + bias_qv[0].reshape(-1)).astype(jnp.bfloat16)
    key_rows = product(hidden_one, qkv_full[1]).astype(jnp.bfloat16)
    value_rows = (product(hidden_one, qkv_full[2]) + bias_qv[1].reshape(-1)).astype(jnp.bfloat16)
    scores = head_scores(query, key_rows, allowed, head_count, head_width)
    row_top = jnp.max(scores, axis=-1, keepdims=True)
    log_total = jnp.log(jnp.sum(jnp.exp(scores - row_top), axis=-1, keepdims=True)) + row_top
    probs_low = jnp.exp(scores - log_total).astype(jnp.bfloat16)
    mixed = jnp.einsum(
        "hqk,khd->qhd",
        probs_low,
        value_rows.reshape(row_count, head_count, head_width),
        preferred_element_type=jnp.float32,
    )
    mixed = mixed.reshape(row_count, -1).astype(jnp.bfloat16)
    partial_attn = product(mixed, out_full)
    resid = rows_in + lax.psum(partial_attn, "mp") + bias_out[0]
    normed_two, scaled_two, inverse_two = normalize(resid, gain_full[1], shift_full[1])
    hidden_two = normed_two.astype(jnp.bfloat16)
    pre = product(hidden_two, up_full) + bias_up.astype(jnp.float32).reshape(-1)
    act = jax.nn.gelu(pre, approximate=False).astype(jnp.bfloat16)
    partial_ffn = product(act, down_full)
    result = (
        resid + lax.psum(partial_ffn.astype(jnp.bfloat16), "mp").astype(jnp.float32) + bias_out[1]
    )
    kept = (
        allowed,
        scaled_one,
        inverse_one,
        hidden_one,
        query,
        key_rows,
        value_rows,
        log_total,
        mixed,
        scaled_two,
        inverse_two,
        hidden_two,
        pre,
        act,
    )
    return (result, kept)


def backward(grad_out, result, kept, weights):
    qkv_full, out_full, up_full, down_full, bias_qv, bias_up, bias_out, gain_full, shift_full = (
        weights
    )
    (
        allowed,
        scaled_one,
        inverse_one,
        hidden_one,
        query,
        key_rows,
        value_rows,
        log_total,
        mixed,
        scaled_two,
        inverse_two,
        hidden_two,
        pre,
        act,
    ) = kept
    head_count = bias_qv.shape[1]
    head_width = bias_qv.shape[2]
    row_count = grad_out.shape[0]
    gain_full = gain_full.astype(jnp.float32)
    grad_low = grad_out.astype(jnp.bfloat16)
    grad_down = product(act.T, grad_low)
    grad_pre = (product(grad_low, down_full.T) * gelu_slope(pre)).astype(jnp.bfloat16)
    grad_bup = jnp.sum(grad_pre, axis=0, dtype=jnp.float32).reshape(bias_up.shape)
    grad_up = product(hidden_two.T, grad_pre)
    partial_two = product(grad_pre, up_full.T)
    grad_two = lax.psum(partial_two.astype(jnp.bfloat16), "mp").astype(jnp.float32)
    gain_two = jnp.sum(grad_two * scaled_two, axis=0)
    shift_two = jnp.sum(grad_two, axis=0)
    grad_resid = grad_out + normalize_back(grad_two, scaled_two, inverse_two, gain_full[1])
    resid_low = grad_resid.astype(jnp.bfloat16)
    grad_out_proj = product(mixed.T, resid_low)
    grad_mixed = (
        product(resid_low, out_full.T)
        .astype(jnp.bfloat16)
        .reshape(row_count, head_count, head_width)
    )
    scores = head_scores(query, key_rows, allowed, head_count, head_width)
    probs = jnp.exp(scores - log_total)
    probs_low = probs.astype(jnp.bfloat16)
    value_heads = value_rows.reshape(row_count, head_count, head_width)
    grad_value = jnp.einsum(
        "hqk,qhd->khd", probs_low, grad_mixed, preferred_element_type=jnp.float32
    ).astype(jnp.bfloat16)
    grad_probs = jnp.einsum(
        "qhd,khd->hqk", grad_mixed, value_heads, preferred_element_type=jnp.float32
    )
    grad_scores = (
        probs * (grad_probs - jnp.sum(grad_probs * probs, axis=-1, keepdims=True))
    ).astype(jnp.bfloat16)
    score_scale = 1.0 / math.sqrt(head_width)
    key_heads = key_rows.reshape(row_count, head_count, head_width)
    query_heads = query.reshape(row_count, head_count, head_width)
    grad_query = (
        jnp.einsum("hqk,khd->qhd", grad_scores, key_heads, preferred_element_type=jnp.float32)
        * score_scale
    ).astype(jnp.bfloat16)
    grad_key = (
        jnp.einsum("hqk,qhd->khd", grad_scores, query_heads, preferred_element_type=jnp.float32)
        * score_scale
    ).astype(jnp.bfloat16)
    stacked = jnp.stack(
        [
            grad_query.reshape(row_count, -1),
            grad_key.reshape(row_count, -1),
            grad_value.reshape(row_count, -1),
        ]
    )
    grad_qkv = jnp.einsum("rd,crk->cdk", hidden_one, stacked, preferred_element_type=jnp.float32)
    partial_one = jnp.einsum("crk,cdk->rd", stacked, qkv_full, preferred_element_type=jnp.float32)
    grad_one = lax.psum(partial_one.astype(jnp.bfloat16), "mp").astype(jnp.float32)
    grad_bqv = jnp.stack(
        [
            jnp.sum(stacked[0], axis=0, dtype=jnp.float32),
            jnp.sum(stacked[2], axis=0, dtype=jnp.float32),
        ]
    ).reshape(2, head_count, head_width)
    gain_one = jnp.sum(grad_one * scaled_one, axis=0)
    shift_one = jnp.sum(grad_one, axis=0)
    grad_in = grad_resid + normalize_back(grad_one, scaled_one, inverse_one, gain_full[0])
    small_sums = jnp.stack(
        [
            jnp.sum(grad_resid, axis=0),
            jnp.sum(grad_out, axis=0),
            gain_one,
            gain_two,
            shift_one,
            shift_two,
        ]
    )
    local_grads = (
        grad_qkv,
        grad_out_proj,
        grad_up,
        grad_down,
        grad_bqv,
        grad_bup,
        small_sums[0:2],
        small_sums[2:4],
        small_sums[4:6],
    )
    return (result, grad_in, local_grads)


def body(
    activations,
    cotangent,
    w_qkv,
    w_o,
    w_up,
    w_down,
    b_qv,
    b_up,
    out_bias,
    norm_gain,
    norm_bias,
    chain_ids,
    key_keep,
):
    batch_count = activations.shape[0]
    outputs = []
    input_grads = []
    running = None
    for batch_index in range(batch_count):
        weights = (
            lax.all_gather(w_qkv, "dp", axis=1, tiled=True),
            lax.all_gather(w_o, "dp", axis=1, tiled=True),
            lax.all_gather(w_up, "dp", axis=0, tiled=True),
            lax.all_gather(w_down, "dp", axis=1, tiled=True),
            lax.all_gather(b_qv, "dp", axis=2, tiled=True),
            lax.all_gather(b_up, "dp", axis=1, tiled=True),
            lax.all_gather(out_bias, "dp", axis=1, tiled=True),
            lax.all_gather(norm_gain, "dp", axis=1, tiled=True),
            lax.all_gather(norm_bias, "dp", axis=1, tiled=True),
        )
        result, kept = forward(
            activations[batch_index].astype(jnp.float32),
            chain_ids[batch_index],
            key_keep[batch_index],
            weights,
        )
        live_rows = (chain_ids[batch_index] >= 0).astype(jnp.float32)[:, None]
        output_rows, grad_in, local_grads = backward(
            cotangent[batch_index].astype(jnp.float32) * live_rows, result, kept, weights
        )
        outputs.append(output_rows)
        input_grads.append(grad_in)
        shares = (
            lax.psum_scatter(
                local_grads[0].astype(jnp.bfloat16), "dp", scatter_dimension=1, tiled=True
            ).astype(jnp.float32),
            lax.psum_scatter(
                local_grads[1].astype(jnp.bfloat16), "dp", scatter_dimension=1, tiled=True
            ).astype(jnp.float32),
            lax.psum_scatter(
                local_grads[2].astype(jnp.bfloat16), "dp", scatter_dimension=0, tiled=True
            ).astype(jnp.float32),
            lax.psum_scatter(
                local_grads[3].astype(jnp.bfloat16), "dp", scatter_dimension=1, tiled=True
            ).astype(jnp.float32),
            lax.psum_scatter(
                local_grads[4].astype(jnp.bfloat16), "dp", scatter_dimension=2, tiled=True
            ).astype(jnp.float32),
            lax.psum_scatter(
                local_grads[5].astype(jnp.bfloat16), "dp", scatter_dimension=1, tiled=True
            ).astype(jnp.float32),
            lax.psum_scatter(
                local_grads[6].astype(jnp.bfloat16), "dp", scatter_dimension=1, tiled=True
            ).astype(jnp.float32),
            lax.psum_scatter(
                local_grads[7].astype(jnp.bfloat16), "dp", scatter_dimension=1, tiled=True
            ).astype(jnp.float32),
            lax.psum_scatter(
                local_grads[8].astype(jnp.bfloat16), "dp", scatter_dimension=1, tiled=True
            ).astype(jnp.float32),
        )
        if running is None:
            running = tuple(shares)
        else:
            running = tuple(jax.tree.map(jnp.add, tuple(running), tuple(shares)))
    return (
        jnp.stack(outputs),
        jnp.stack(input_grads),
        running[0],
        running[1],
        running[2],
        running[3],
        running[4],
        running[5],
        running[6],
        running[7],
        running[8],
    )


def solution(mesh):
    placed = (
        P(None, "dp", None),
        P(None, "dp", None),
        P(None, "dp", "mp"),
        P("mp", "dp"),
        P("dp", "mp"),
        P("mp", "dp"),
        P(None, "mp", "dp"),
        P("mp", "dp"),
        P(None, "dp"),
        P(None, "dp"),
        P(None, "dp"),
        P(None, "dp"),
        P(None, "dp"),
    )
    return jax.shard_map(
        body,
        mesh=mesh,
        in_specs=placed,
        out_specs=(
            P(None, "dp", None),
            P(None, "dp", None),
            P(None, "dp", "mp"),
            P("mp", "dp"),
            P("dp", "mp"),
            P("mp", "dp"),
            P(None, "mp", "dp"),
            P("mp", "dp"),
            P(None, "dp"),
            P(None, "dp"),
            P(None, "dp"),
        ),
        check_vma=False,
    )
```

profile of v0, /device:TPU:0, one launch (start us, length us, event | category | flops | bytes accessed | tf_op | source)
XLA Modules:
  0.0 1243.1 jit_solution(9962415222344937010)
XLA Ops:
  9.0 23.3 %all-gather = bf16[16,32,2]{1,2,0:T(2,128)(2,1)S(1)} all-gather(bf16[1,32,2]{1,2,0:T(2,128)(2,1)} %bitcast.362), channel_id=1, replica_groups=mesh['dp'=16,'mp'=2] {'dp'}, dimensions={0}, use_global_device_ids=true | all-gather | bytes 2176 | tf_op jit(solution)/shard_map/all_gather | solution.py:249
  32.4 17.6 %all-gather.1 = bf16[16,32,2]{1,2,0:T(2,128)(2,1)S(1)} all-gather(bf16[1,32,2]{1,2,0:T(2,128)(2,1)} %bitcast.363), channel_id=1, replica_groups=mesh['dp'=16,'mp'=2] {'dp'}, dimensions={0}, use_global_device_ids=true | all-gather | bytes 2176 | tf_op jit(solution)/shard_map/all_gather | solution.py:250
  54.5 18.8 %all_gather.39 = bf16[2,4,64]{1,0,2:T(2,128)(2,1)S(1)} all-gather(bf16[2,4,4]{1,0,2:T(2,128)(2,1)S(1)} %copy.117), channel_id=1, replica_groups=mesh['dp'=16,'mp'=2] {'dp'}, dimensions={2}, use_global_device_ids=true | all-gather | bytes 1088 | tf_op jit(solution)/shard_map/all_gather | solution.py:246
  73.7 19.6 %all_gather.38 = bf16[3,512,256]{2,1,0:T(8,128)(2,1)S(1)} all-gather(bf16[3,32,256]{2,1,0:T(8,128)(2,1)S(1)} %copy-done.61), channel_id=1, replica_groups=mesh['dp'=16,'mp'=2] {'dp'}, dimensions={1}, use_global_device_ids=true | all-gather | bytes 835584 | tf_op jit(solution)/shard_map/all_gather | solution.py:242
  99.8 19.8 %all_gather.40 = bf16[256,512]{0,1:T(8,128)(2,1)S(1)} all-gather(bf16[256,32]{0,1:T(8,128)(2,1)S(1)} %copy-done.64), channel_id=1, replica_groups=mesh['dp'=16,'mp'=2] {'dp'}, dimensions={1}, use_global_device_ids=true | all-gather | bytes 278528 | tf_op jit(solution)/shard_map/all_gather | solution.py:243
  138.2 10.3 convolution_convert_fusion.14
  158.8 17.4 %all-gather.2 = bf16[16,32,2]{1,2,0:T(2,128)(2,1)S(1)} all-gather(bf16[1,32,2]{1,2,0:T(2,128)(2,1)S(1)} %bitcast.364), channel_id=1, replica_groups=mesh['dp'=16,'mp'=2] {'dp'}, dimensions={0}, use_global_device_ids=true | all-gather | bytes 2176 | tf_op jit(solution)/shard_map/all_gather | solution.py:248
  176.9 19.3 %all-gather.3 = bf16[16,4,16]{2,1,0:T(4,128)(2,1)S(1)} all-gather(bf16[1,4,16]{2,1,0:T(4,128)(2,1)S(1)} %bitcast.359), channel_id=1, replica_groups=mesh['dp'=16,'mp'=2] {'dp'}, dimensions={0}, use_global_device_ids=true | all-gather | bytes 2176 | tf_op jit(solution)/shard_map/all_gather | solution.py:247
  196.3 66.6 %all-reduce.16.cloned.1.call-done = (f32[1024,512]{1,0:T(8,128)}, f32[1024,512]{1,0:T(8,128)}) async-done(((f32[1024,512]{1,0:T(8,128)}, f32[1024,512]{1,0:T(8,128)}), (f32[1024,512]{1,0:T(8,128)}, f32[1024,512]{1,0:T(8,128)})) %all-reduce.16.cloned.1.call-update) | async-done | bytes 4194320 | tf_op jit(solution)/shard_map/psum | solution.py:85
  267.8 5.3 fusion.149
  273.2 5.7 fusion.163
  283.5 21.0 %fusion.6 = (bf16[1024,1024]{1,0:T(8,128)(2,1)}, bf16[1024,1024]{1,0:T(8,128)(2,1)}, f32[1024,1024]{1,0:T(8,128)S(1)}) fusion(f32[1024]{0:T(1024)S(1)} %reshape.484, f32[1024,1024]{1,0:T(8,128)S(1)} %copy-done.85, bf16[512,1024]{1,0:T(8,128)(2,1)S(1)} %copy-done.83, f32[1024,512]{1,0:T(8,128)S(1)} %copy-done.5, f32[512]{0:T(512)S(1)} %bitcast.356, ...), kind=kOutput, calls=%fused_computation.20 | convolution fusion | flops 1214775296 | bytes 15745024 | tf_op jit(solution)/shard_map/dot_general | solution.py:12
  312.0 4.7 convolution_convert_fusion.2
  334.3 40.7 %all-reduce.22.cloned.1.call-done = (bf16[1024,512]{1,0:T(8,128)(2,1)}, bf16[1024,512]{1,0:T(8,128)(2,1)}) async-done(((bf16[1024,512]{1,0:T(8,128)(2,1)}, bf16[1024,512]{1,0:T(8,128)(2,1)}), (bf16[1024,512]{1,0:T(8,128)(2,1)}, bf16[1024,512]{1,0:T(8,128)(2,1)})) %all-reduce.22.cloned.1.call-update) | async-done | bytes 2097168 | tf_op jit(solution)/shard_map/psum | solution.py:143
  378.3 6.3 fusion.104
  389.1 16.5 %multiply_reduce_fusion.1 = (f32[4,1024]{1,0:T(4,128)}, f32[4,1024,1024]{1,2,0:T(8,128)}) fusion(f32[4,1024,1024]{1,2,0:T(8,128)} %copy-done, f32[4,1024]{1,0:T(4,128)} %copy-done.49, pred[1024,1024]{0,1:T(8,128)(4,1)S(1)} %get-tuple-element.158, bf16[1024,4,64]{0,2,1:T(8,128)(2,1)} %bitcast.297, bf16[1024,4,64]{0,2,1:T(8,128)(2,1)} %bitcast.311), kind=kOutput, calls=%fused_computation.3 | convolution fusion | flops 557838336 | bytes 35684352 | tf_op jit(solution)/shard_map/qhd,khd->hqk/dot_general | solution.py:161
  405.6 8.3 multiply_convert_fusion.1
  421.0 9.7 bitcast_reduce_fusion
  430.8 12.4 multiply_reduce_fusion
  444.0 12.7 %multiply_convert_fusion = bf16[4,1024,1024]{1,2,0:T(8,128)(2,1)S(1)} fusion(f32[4,1024,1024]{1,2,0:T(8,128)} %get-tuple-element.141, f32[4,1024,1024]{1,2,0:T(8,128)} %copy-done.1, f32[4,1024]{1,0:T(4,128)S(1)} %get-tuple-element.140, f32[4,1024]{1,0:T(4,128)S(1)} %copy-done.52, pred[1024,1024]{0,1:T(8,128)(4,1)S(1)} %copy-done.9), kind=kLoop, calls=%fused_computation | loop fusion | flops 25165824 | bytes 43024384 | tf_op jit(solution)/shard_map/convert_element_type | solution.py:166
  463.2 9.7 bitcast_reduce_fusion.2
  510.7 44.8 %reduce-scatter.37.cloned.1.call-done = bf16[1024,32]{0,1:T(8,128)(2,1)} async-done(((bf16[1024,512]{0,1:T(8,128)(2,1)}), bf16[1024,32]{0,1:T(8,128)(2,1)}) %reduce-scatter.37.cloned.1.call-update) | async-done | bytes 65552 | tf_op jit(solution)/shard_map/reduce_scatter | solution.py:274
  558.8 57.7 %all-reduce.7 = (bf16[2,4,64]{2,1,0:T(4,128)(2,1)S(1)}, bf16[2,4,64]{2,1,0:T(4,128)(2,1)S(1)}, bf16[16,64]{1,0:T(8,128)(2,1)S(1)}, bf16[16,64]{1,0:T(8,128)(2,1)S(1)}) all-reduce(bf16[2,4,64]{2,1,0:T(4,128)(2,1)S(1)} %pad_maximum_fusion.9, ...), channel_id=11, replica_groups=mesh['dp'=16,'mp'=2] {'dp'}, use_global_device_ids=true, to_apply=%region_43.44.clone | all-reduce | flops 3072 | bytes 12288
  618.6 52.8 %reduce-scatter.41.cloned.1.call-done = bf16[32,2]{1,0:T(8,128)(2,1)} async-done(((bf16[512,2]{1,0:T(8,128)(2,1)}), bf16[32,2]{1,0:T(8,128)(2,1)}) %reduce-scatter.41.cloned.1.call-update) | async-done | bytes 144
  672.8 56.9 %reduce-scatter.31.cloned.1.call-done = bf16[256,32]{0,1:T(8,128)(2,1)} async-done(((bf16[256,512]{0,1:T(8,128)(2,1)}), bf16[256,32]{0,1:T(8,128)(2,1)}) %reduce-scatter.31.cloned.1.call-update) | async-done | bytes 16400 | tf_op jit(solution)/shard_map/reduce_scatter | solution.py:268
  729.7 58.4 %reduce-scatter.29.cloned.1.call-done = bf16[256,32]{0,1:T(8,128)(2,1)} async-done(((bf16[256,512]{0,1:T(8,128)(2,1)}), bf16[256,32]{0,1:T(8,128)(2,1)}) %reduce-scatter.29.cloned.1.call-update) | async-done | bytes 16400 | tf_op jit(solution)/shard_map/reduce_scatter | solution.py:268
  789.4 99.1 %all-reduce.18.cloned.1.call-done = (bf16[3,512,256]{2,0,1:T(4,128)(2,1)}, bf16[3,512,256]{2,0,1:T(4,128)(2,1)}) async-done(((bf16[3,512,256]{2,0,1:T(4,128)(2,1)}, bf16[3,512,256]{2,0,1:T(4,128)(2,1)}), (bf16[3,512,256]{2,0,1:T(4,128)(2,1)}, bf16[3,512,256]{2,0,1:T(4,128)(2,1)})) %all-reduce.18.cloned.1.call-update) | async-done | bytes 1572880
  890.1 108.0 %all-reduce.20.cloned.1.call-done = (bf16[1024,512]{1,0:T(8,128)(2,1)}, bf16[1024,512]{1,0:T(8,128)(2,1)}, bf16[1024,512]{1,0:T(8,128)(2,1)}, bf16[1024,512]{1,0:T(8,128)(2,1)}) async-done(((bf16[1024,512]{1,0:T(8,128)(2,1)}, bf16[1024,512]{1,0:T(8,128)(2,1)}, bf16[1024,512]{1,0:T(8,128)(2,1)}, bf16[1024,512]{1,0:T(8,128)(2,1)}), (bf16[1024,512]{1,0:T(8,128)(2,1)}, bf16[1024,512]{1,0:T(8,128)(2,1)}, ...) | async-done | bytes 4194320 | tf_op jit(solution)/shard_map/psum | solution.py:92
  1019.6 39.0 %reduce-scatter.45.cloned.1.call-done = bf16[32,2]{1,0:T(8,128)(2,1)} async-done(((bf16[512,2]{1,0:T(8,128)(2,1)}), bf16[32,2]{1,0:T(8,128)(2,1)}) %reduce-scatter.45.cloned.1.call-update) | async-done | bytes 144
  1059.4 57.4 %reduce-scatter.47.cloned.1.call-done = bf16[32,2]{1,0:T(8,128)(2,1)} async-done(((bf16[512,2]{1,0:T(8,128)(2,1)}), bf16[32,2]{1,0:T(8,128)(2,1)}) %reduce-scatter.47.cloned.1.call-update) | async-done | bytes 144
  1117.6 57.4 %reduce-scatter.49.cloned.1.call-done = bf16[32,2]{1,0:T(8,128)(2,1)} async-done(((bf16[512,2]{1,0:T(8,128)(2,1)}), bf16[32,2]{1,0:T(8,128)(2,1)}) %reduce-scatter.49.cloned.1.call-update) | async-done | bytes 144
  1175.7 57.4 %reduce-scatter.51.cloned.1.call-done = bf16[32,2]{1,0:T(8,128)(2,1)} async-done(((bf16[512,2]{1,0:T(8,128)(2,1)}), bf16[32,2]{1,0:T(8,128)(2,1)}) %reduce-scatter.51.cloned.1.call-update) | async-done | bytes 144
  (369 shorter events, 169.6 us)
Async XLA Ops:
  8.0 85.3 %copy-start.2 = (bf16[2,1024,512]{2,1,0:T(8,128)(2,1)S(1)}, bf16[2,1024,512]{2,1,0:T(8,128)(2,1)}, u32[]{:S(2)}) copy-start(bf16[2,1024,512]{2,1,0:T(8,128)(2,1)} %param.13) | copy-start | bytes 6291460
  8.0 65.6 %copy-start.61 = (bf16[3,32,256]{2,1,0:T(8,128)(2,1)S(1)}, bf16[3,32,256]{2,1,0:T(8,128)(2,1)}, u32[]{:S(2)}) copy-start(bf16[3,32,256]{2,1,0:T(8,128)(2,1)} %param.15) | copy-start | bytes 147460
  8.0 254.9 %all-reduce.16.cloned.1.call-start = ((), (), s32[]{:S(2)}) async-start(), calls=%async_computation.26 | async-start | bytes 8388608 | tf_op jit(solution)/shard_map/psum | solution.py:85
  32.4 61.9 %copy-start.62 = (f32[1,512]{1,0:T(1,128)}, f32[1,512]{1,0:T(1,128)S(1)}, u32[]{:S(2)}) copy-start(f32[1,512]{1,0:T(1,128)S(1)} %get-tuple-element.127) | copy-start | bytes 6148
  50.1 44.2 %copy-start.65 = (f32[1,512]{1,0:T(1,128)}, f32[1,512]{1,0:T(1,128)S(1)}, u32[]{:S(2)}) copy-start(f32[1,512]{1,0:T(1,128)S(1)} %get-tuple-element.129) | copy-start | bytes 6148
  52.0 42.8 %copy-start.53 = (f32[1024]{0:T(1024)}, f32[1024]{0:T(1024)S(1)}, u32[]{:S(2)}) copy-start(f32[1024]{0:T(1024)S(1)} %get-tuple-element.156) | copy-start | bytes 12292
  52.0 42.7 %copy-start.55 = (f32[1024]{0:T(1024)}, f32[1024]{0:T(1024)S(1)}, u32[]{:S(2)}) copy-start(f32[1024]{0:T(1024)S(1)} %get-tuple-element.157) | copy-start | bytes 12292
  119.6 266.8 %copy-start.15 = (bf16[256,512]{0,1:T(8,128)(2,1)}, bf16[256,512]{0,1:T(8,128)(2,1)S(1)}, u32[]{:S(2)}) copy-start(bf16[256,512]{0,1:T(8,128)(2,1)S(1)} %all_gather.40) | copy-start | bytes 786436
  157.6 110.2 %all-gather.7.cloned.1.call-start = ((), (), s32[]{:S(2)}) async-start(), calls=%async_computation.12 | async-start | bytes 1114112 | tf_op jit(solution)/shard_map/all_gather | solution.py:244
  158.1 115.0 %all-gather.9.cloned.1.call-start = ((), (), s32[]{:S(2)}) async-start(), calls=%async_computation.13 | async-start | bytes 1114112 | tf_op jit(solution)/shard_map/all_gather | solution.py:245
  158.7 216.3 %all-reduce.22.cloned.1.call-start = ((), (), s32[]{:S(2)}) async-start(), calls=%async_computation.29 | async-start | bytes 4194304 | tf_op jit(solution)/shard_map/psum | solution.py:143
  311.9 197.2 %reduce-scatter.35.cloned.1.call-start = ((), (), s32[]{:S(2)}) async-start(), calls=%async_computation.17 | async-start | bytes 1114112 | tf_op jit(solution)/shard_map/reduce_scatter | solution.py:271
  316.7 192.5 %reduce-scatter.33.cloned.1.call-start = ((), (), s32[]{:S(2)}) async-start(), calls=%async_computation.16 | async-start | bytes 1114112 | tf_op jit(solution)/shard_map/reduce_scatter | solution.py:271
  321.2 189.5 %reduce-scatter.39.cloned.1.call-start = ((), (), s32[]{:S(2)}) async-start(), calls=%async_computation.19 | async-start | bytes 1114112 | tf_op jit(solution)/shard_map/reduce_scatter | solution.py:274
  325.6 229.9 %reduce-scatter.37.cloned.1.call-start = ((), (), s32[]{:S(2)}) async-start(), calls=%async_computation.18 | async-start | bytes 1114112 | tf_op jit(solution)/shard_map/reduce_scatter | solution.py:274
  330.0 287.8 %reduce-scatter.43.cloned.1.call-start = ((), (), s32[]{:S(2)}) async-start(), calls=%async_computation.21 | async-start | bytes 139264
  473.0 198.5 %reduce-scatter.41.cloned.1.call-start = ((), (), s32[]{:S(2)}) async-start(), calls=%async_computation.20 | async-start | bytes 139264
  473.9 255.8 %reduce-scatter.31.cloned.1.call-start = ((), (), s32[]{:S(2)}) async-start(), calls=%async_computation.15 | async-start | bytes 278528 | tf_op jit(solution)/shard_map/reduce_scatter | solution.py:268
  481.1 306.9 %reduce-scatter.29.cloned.1.call-start = ((), (), s32[]{:S(2)}) async-start(), calls=%async_computation.14 | async-start | bytes 278528 | tf_op jit(solution)/shard_map/reduce_scatter | solution.py:268
  494.5 394.0 %all-reduce.18.cloned.1.call-start = ((), (), s32[]{:S(2)}) async-start(), calls=%async_computation.27 | async-start | bytes 4194304
  498.4 499.7 %all-reduce.20.cloned.1.call-start = ((), (), s32[]{:S(2)}) async-start(), calls=%async_computation.28 | async-start | bytes 8388608 | tf_op jit(solution)/shard_map/psum | solution.py:92
  504.9 52.1 %copy-start.12 = (bf16[1024,512]{1,0:T(8,128)(2,1)S(1)}, bf16[1024,512]{1,0:T(8,128)(2,1)}, u32[]{:S(2)}) copy-start(bf16[1024,512]{1,0:T(8,128)(2,1)} %get-tuple-element.100) | copy-start | bytes 3145732
  507.0 51.7 %copy-start.70 = (bf16[512]{0:T(512)(128)(2,1)S(1)}, bf16[512]{0:T(512)(128)(2,1)}, u32[]{:S(2)}) copy-start(bf16[512]{0:T(512)(128)(2,1)} %get-tuple-element.132) | copy-start | bytes 3076
  507.0 51.7 %copy-start.73 = (bf16[4,64]{1,0:T(4,128)(2,1)S(1)}, bf16[4,64]{1,0:T(4,128)(2,1)}, u32[]{:S(2)}) copy-start(bf16[4,64]{1,0:T(4,128)(2,1)} %get-tuple-element.150) | copy-start | bytes 1540
  507.0 51.7 %copy-start.80 = (bf16[4,64]{1,0:T(4,128)(2,1)S(1)}, bf16[4,64]{1,0:T(4,128)(2,1)}, u32[]{:S(2)}) copy-start(bf16[4,64]{1,0:T(4,128)(2,1)} %get-tuple-element.148) | copy-start | bytes 1540
  507.0 51.8 %copy-start.74 = (bf16[4,64]{1,0:T(4,128)(2,1)S(1)}, bf16[4,64]{1,0:T(4,128)(2,1)}, u32[]{:S(2)}) copy-start(bf16[4,64]{1,0:T(4,128)(2,1)} %get-tuple-element.146) | copy-start | bytes 1540
  507.0 51.8 %copy-start.79 = (bf16[4,64]{1,0:T(4,128)(2,1)S(1)}, bf16[4,64]{1,0:T(4,128)(2,1)}, u32[]{:S(2)}) copy-start(bf16[4,64]{1,0:T(4,128)(2,1)} %get-tuple-element.144) | copy-start | bytes 1540
  507.0 495.9 %copy-start.69 = (f32[1,512]{1,0:T(1,128)S(1)}, f32[1,512]{1,0:T(1,128)}, u32[]{:S(2)}) copy-start(f32[1,512]{1,0:T(1,128)} %get-tuple-element.122) | copy-start | bytes 6148
  507.0 551.6 %reduce-scatter.45.cloned.1.call-start = ((), (), s32[]{:S(2)}) async-start(), calls=%async_computation.22 | async-start | bytes 139264
  1002.9 113.9 %reduce-scatter.47.cloned.1.call-start = ((), (), s32[]{:S(2)}) async-start(), calls=%async_computation.23 | async-start | bytes 139264
  1011.0 163.9 %reduce-scatter.49.cloned.1.call-start = ((), (), s32[]{:S(2)}) async-start(), calls=%async_computation.24 | async-start | bytes 139264
  1012.1 221.0 %reduce-scatter.51.cloned.1.call-start = ((), (), s32[]{:S(2)}) async-start(), calls=%async_computation.25 | async-start | bytes 139264
  (78 other events, 682.3 us)
Sparse Core Ops, SparseCore 0:
  157.7 105.1 all-reduce.15
  312.0 62.9 all-reduce.21
Sparse Core Ops, SparseCore 1:
  160.2 35.0 all-gather.6
  197.3 36.8 all-gather.8
  316.8 57.6 reduce-scatter.34
  378.1 56.6 reduce-scatter.32
  438.4 56.7 reduce-scatter.38
  498.8 56.6 reduce-scatter.36
  558.8 54.6 reduce-scatter.42
  616.8 54.6 reduce-scatter.40
  674.8 54.8 reduce-scatter.30
  733.2 54.8 reduce-scatter.28
  791.5 96.9 all-reduce.17
  891.1 107.0 all-reduce.19
  1003.0 55.6 reduce-scatter.44
  1062.1 54.6 reduce-scatter.46
  1120.3 54.6 reduce-scatter.48
  1178.4 54.7 reduce-scatter.50
where the time goes:
time: 1250 us; the launch traced here: 1240 us
  waiting for transfers between devices  740 us (59%)
  blocking collectives  193 us (15%)
  matrix products  176 us (14%)
  other arithmetic  78.4 us (6%)
  local copies, waits for them, and re-layouts  35.5 us (3%)
  between operations  18.9 us (2%)
    unnamed x25, waiting for transfers between devices  364 us
    reduce_scatter x2, waiting for transfers between devices, body(): lax.psum_scatter(local_grads[1].astype(jnp.bfloat16), 'dp', scatter_dimen...  115 us
    psum x1, waiting for transfers between devices, forward(): lax.psum(partial_ffn.astype(jnp.bfloat16), 'mp').astype(jnp.float32)  108 us
    dot_general x24, matrix products, product(): return jnp.dot(left, right, preferred_element_type=jnp.float32)  83.6 us
    psum x1, waiting for transfers between devices, forward(): resid = rows_in + lax.psum(partial_attn, 'mp') + bias_out[0]  66.6 us
    unnamed x1, blocking collectives  57.7 us
    reduce_scatter x2, waiting for transfers between devices, body(): lax.psum_scatter(local_grads[3].astype(jnp.bfloat16), 'dp', scatter_dimen...  44.8 us
    psum x1, waiting for transfers between devices, backward(): lax.psum(partial_two.astype(jnp.bfloat16), 'mp').astype(jnp.float32)  40.7 us
  transfers between devices with their start and end apart: 18, of which 12 were waited for; matrix products, arithmetic and copies ran while one was open for 15% of the time, Pallas kernels for 0%

commit v1 on v0

--- a/solution.py
+++ b/solution.py
@@ -89,7 +89,11 @@
     act = jax.nn.gelu(pre, approximate=False).astype(jnp.bfloat16)
     partial_ffn = product(act, down_full)
     result = (
-        resid + lax.psum(partial_ffn.astype(jnp.bfloat16), "mp").astype(jnp.float32) + bias_out[1]
+        resid
+        + jnp.sum(lax.all_gather(partial_ffn.astype(jnp.bfloat16), "mp"), axis=0).astype(
+            jnp.float32
+        )
+        + bias_out[1]
     )
     kept = (
         allowed,

time: 1250 us -> 1210 us (0.968)
  waiting for transfers between devices: 740 us -> 690 us
    all_gather x0 -> x2, waiting for transfers between devices: none -> 62.9 us  [forward(): lax.all_gather(partial_ffn.astype(jnp.bfloat16), 'mp')]
    psum x1, waiting for transfers between devices: 108 us -> 62.9 us  [backward(): lax.psum(partial_one.astype(jnp.bfloat16), 'mp').astype(jnp.float32)]
    reduce_scatter x2, waiting for transfers between devices: 44.8 us -> 0.01 us  [body(): lax.psum_scatter(local_grads[3].astype(jnp.bfloat16), 'dp', scatter_dimen...]
    unnamed x25 -> x27, waiting for transfers between devices: 364 us -> 345 us
  transfers between devices with their start and end apart: 18 -> 20, of which waited for: 12 -> 13; matrix products, arithmetic and copies ran while one was open for 15% -> 17% of each run, Pallas kernels for 0% -> 0%
where the time goes in v1:
time: 1210 us
  waiting for transfers between devices  690 us (57%)
  blocking collectives  197 us (16%)
  matrix products  178 us (15%)
  other arithmetic  86.4 us (7%)
  local copies, waits for them, and re-layouts  35.7 us (3%)
  between operations  18.4 us (2%)
    unnamed x27, waiting for transfers between devices  345 us
    reduce_scatter x2, waiting for transfers between devices, body(): lax.psum_scatter(local_grads[1].astype(jnp.bfloat16), 'dp', scatter_dimen...  115 us
    dot_general x24, matrix products, product(): return jnp.dot(left, right, preferred_element_type=jnp.float32)  83.2 us
    psum x1, waiting for transfers between devices, forward(): resid = rows_in + lax.psum(partial_attn, 'mp') + bias_out[0]  67.4 us
    all_gather x2, waiting for transfers between devices, forward(): lax.all_gather(partial_ffn.astype(jnp.bfloat16), 'mp')  62.9 us
    psum x1, waiting for transfers between devices, backward(): lax.psum(partial_one.astype(jnp.bfloat16), 'mp').astype(jnp.float32)  62.9 us
    unnamed x1, blocking collectives  61.2 us
    psum x1, waiting for transfers between devices, backward(): lax.psum(partial_two.astype(jnp.bfloat16), 'mp').astype(jnp.float32)  36.3 us
  transfers between devices with their start and end apart: 20, of which 13 were waited for; matrix products, arithmetic and copies ran while one was open for 17% of the time, Pallas kernels for 0%

profile of v1, /device:TPU:0, one launch (start us, length us, event | category | flops | bytes accessed | tf_op | source)
XLA Modules:
  0.0 1206.2 jit_solution(2706881742712626171)
XLA Ops:
  9.0 23.3 %all-gather.2 = bf16[16,32,2]{1,2,0:T(2,128)(2,1)S(1)} all-gather(bf16[1,32,2]{1,2,0:T(2,128)(2,1)} %bitcast.367), channel_id=1, replica_groups=mesh['dp'=16,'mp'=2] {'dp'}, dimensions={0}, use_global_device_ids=true | all-gather | bytes 2176 | tf_op jit(solution)/shard_map/all_gather | solution.py:253
  32.4 17.6 %all-gather.3 = bf16[16,32,2]{1,2,0:T(2,128)(2,1)S(1)} all-gather(bf16[1,32,2]{1,2,0:T(2,128)(2,1)} %bitcast.368), channel_id=1, replica_groups=mesh['dp'=16,'mp'=2] {'dp'}, dimensions={0}, use_global_device_ids=true | all-gather | bytes 2176 | tf_op jit(solution)/shard_map/all_gather | solution.py:254
  54.5 18.8 %all_gather.51 = bf16[2,4,64]{1,0,2:T(2,128)(2,1)S(1)} all-gather(bf16[2,4,4]{1,0,2:T(2,128)(2,1)S(1)} %copy.117), channel_id=1, replica_groups=mesh['dp'=16,'mp'=2] {'dp'}, dimensions={2}, use_global_device_ids=true | all-gather | bytes 1088 | tf_op jit(solution)/shard_map/all_gather | solution.py:250
  73.7 19.6 %all_gather.50 = bf16[3,512,256]{2,1,0:T(8,128)(2,1)S(1)} all-gather(bf16[3,32,256]{2,1,0:T(8,128)(2,1)S(1)} %copy-done.57), channel_id=1, replica_groups=mesh['dp'=16,'mp'=2] {'dp'}, dimensions={1}, use_global_device_ids=true | all-gather | bytes 835584 | tf_op jit(solution)/shard_map/all_gather | solution.py:246
  99.8 20.0 %all_gather.52 = bf16[256,512]{0,1:T(8,128)(2,1)S(1)} all-gather(bf16[256,32]{0,1:T(8,128)(2,1)S(1)} %copy-done.60), channel_id=1, replica_groups=mesh['dp'=16,'mp'=2] {'dp'}, dimensions={1}, use_global_device_ids=true | all-gather | bytes 278528 | tf_op jit(solution)/shard_map/all_gather | solution.py:247
  138.4 10.3 convolution_convert_fusion.14
  159.0 17.5 %all-gather.4 = bf16[16,32,2]{1,2,0:T(2,128)(2,1)S(1)} all-gather(bf16[1,32,2]{1,2,0:T(2,128)(2,1)S(1)} %bitcast.369), channel_id=1, replica_groups=mesh['dp'=16,'mp'=2] {'dp'}, dimensions={0}, use_global_device_ids=true | all-gather | bytes 2176 | tf_op jit(solution)/shard_map/all_gather | solution.py:252
  176.6 19.0 %all-gather.5 = bf16[16,4,16]{2,1,0:T(4,128)(2,1)S(1)} all-gather(bf16[1,4,16]{2,1,0:T(4,128)(2,1)S(1)} %bitcast.364), channel_id=1, replica_groups=mesh['dp'=16,'mp'=2] {'dp'}, dimensions={0}, use_global_device_ids=true | all-gather | bytes 2176 | tf_op jit(solution)/shard_map/all_gather | solution.py:251
  195.7 67.4 %all-reduce.16.cloned.1.call-done = (f32[1024,512]{1,0:T(8,128)}, f32[1024,512]{1,0:T(8,128)}) async-done(((f32[1024,512]{1,0:T(8,128)}, f32[1024,512]{1,0:T(8,128)}), (f32[1024,512]{1,0:T(8,128)}, f32[1024,512]{1,0:T(8,128)})) %all-reduce.16.cloned.1.call-update) | async-done | bytes 4194320 | tf_op jit(solution)/shard_map/psum | solution.py:85
  268.0 5.3 fusion.149
  273.4 5.7 fusion.163
  283.6 21.0 %fusion.6 = (bf16[1024,1024]{1,0:T(8,128)(2,1)}, bf16[1024,1024]{1,0:T(8,128)(2,1)}, f32[1024,1024]{1,0:T(8,128)S(1)}) fusion(f32[1024]{0:T(1024)S(1)} %reshape.484, f32[1024,1024]{1,0:T(8,128)S(1)} %copy-done.79, bf16[512,1024]{1,0:T(8,128)(2,1)S(1)} %copy-done.77, f32[1024,512]{1,0:T(8,128)S(1)} %copy-done.7, f32[512]{0:T(512)S(1)} %bitcast.361, ...), kind=kOutput, calls=%fused_computation.20 | convolution fusion | flops 1214775296 | bytes 15745024 | tf_op jit(solution)/shard_map/dot_general | solution.py:12
  338.7 36.3 %all-reduce.22.cloned.1.call-done = (bf16[1024,512]{1,0:T(8,128)(2,1)}, bf16[1024,512]{1,0:T(8,128)(2,1)}) async-done(((bf16[1024,512]{1,0:T(8,128)(2,1)}, bf16[1024,512]{1,0:T(8,128)(2,1)}), (bf16[1024,512]{1,0:T(8,128)(2,1)}, bf16[1024,512]{1,0:T(8,128)(2,1)})) %all-reduce.22.cloned.1.call-update) | async-done | bytes 2097168 | tf_op jit(solution)/shard_map/psum | solution.py:147
  378.2 31.6 %all-gather.17.cloned.1.call-done = bf16[2048,512]{1,0:T(8,128)(2,1)} async-done(((bf16[1024,512]{1,0:T(8,128)(2,1)}), bf16[2048,512]{1,0:T(8,128)(2,1)}) %all-gather.17.cloned.1.call-update) | async-done | bytes 2097168 | tf_op jit(solution)/shard_map/all_gather | solution.py:93
  413.0 31.3 %all-gather.15.cloned.1.call-done = bf16[2048,512]{1,0:T(8,128)(2,1)} async-done(((bf16[1024,512]{1,0:T(8,128)(2,1)}), bf16[2048,512]{1,0:T(8,128)(2,1)}) %all-gather.15.cloned.1.call-update) | async-done | bytes 2097168 | tf_op jit(solution)/shard_map/all_gather | solution.py:93
  447.5 7.9 fusion.104
  460.9 16.2 %multiply_reduce_fusion.1 = (f32[4,1024]{1,0:T(4,128)}, f32[4,1024,1024]{1,2,0:T(8,128)}) fusion(f32[4,1024,1024]{1,2,0:T(8,128)} %copy-done, f32[4,1024]{1,0:T(4,128)} %copy-done.45, pred[1024,1024]{0,1:T(8,128)(4,1)S(1)} %get-tuple-element.156, bf16[1024,4,64]{0,2,1:T(8,128)(2,1)} %bitcast.299, bf16[1024,4,64]{0,2,1:T(8,128)(2,1)} %bitcast.315), kind=kOutput, calls=%fused_computation.3 | convolution fusion | flops 557838336 | bytes 35684352 | tf_op jit(solution)/shard_map/qhd,khd->hqk/dot_general | solution.py:165
  477.2 8.4 multiply_convert_fusion.1
  492.6 9.7 bitcast_reduce_fusion
  502.4 12.3 %multiply_reduce_fusion = (f32[4,1024]{1,0:T(4,128)S(1)}, f32[4,1024,1024]{1,2,0:T(8,128)}) fusion(f32[4,1024,1024]{1,2,0:T(8,128)} %copy-done.1, f32[4,1024]{1,0:T(4,128)S(1)} %copy-done.48, pred[1024,1024]{0,1:T(8,128)(4,1)S(1)} %copy-done.5, bf16[1024,4,64]{0,2,1:T(8,128)(2,1)S(1)} %bitcast.302, bf16[1024,4,64]{0,2,1:T(8,128)(2,1)S(1)} %bitcast.314), kind=kOutput, calls=%fused_computation.1 | convolution fusion | flops 557838336 | bytes 35684352 | tf_op jit(solution)/shard_map/qhd,khd->hqk/dot_general | solution.py:165
  515.6 12.6 %multiply_convert_fusion = bf16[4,1024,1024]{1,2,0:T(8,128)(2,1)S(1)} fusion(f32[4,1024,1024]{1,2,0:T(8,128)} %get-tuple-element.139, f32[4,1024,1024]{1,2,0:T(8,128)} %copy-done.1, f32[4,1024]{1,0:T(4,128)S(1)} %get-tuple-element.138, f32[4,1024]{1,0:T(4,128)S(1)} %copy-done.48, pred[1024,1024]{0,1:T(8,128)(4,1)S(1)} %copy-done.5), kind=kLoop, calls=%fused_computation | loop fusion | flops 25165824 | bytes 43024384 | tf_op jit(solution)/shard_map/convert_element_type | solution.py:170
  534.6 9.6 bitcast_reduce_fusion.2
  584.3 61.2 %all-reduce.7 = (bf16[2,4,64]{2,1,0:T(4,128)(2,1)S(1)}, bf16[2,4,64]{2,1,0:T(4,128)(2,1)S(1)}, bf16[16,64]{1,0:T(8,128)(2,1)S(1)}, bf16[16,64]{1,0:T(8,128)(2,1)S(1)}) all-reduce(bf16[2,4,64]{2,1,0:T(4,128)(2,1)S(1)} %pad_maximum_fusion.9, ...), channel_id=13, replica_groups=mesh['dp'=16,'mp'=2] {'dp'}, use_global_device_ids=true, to_apply=%region_43.44.clone | all-reduce | flops 3072 | bytes 12288
  652.3 27.9 %reduce-scatter.43.cloned.1.call-done = bf16[32,2]{1,0:T(8,128)(2,1)} async-done(((bf16[512,2]{1,0:T(8,128)(2,1)}), bf16[32,2]{1,0:T(8,128)(2,1)}) %reduce-scatter.43.cloned.1.call-update) | async-done | bytes 144
  681.6 56.9 %reduce-scatter.31.cloned.1.call-done = bf16[256,32]{0,1:T(8,128)(2,1)} async-done(((bf16[256,512]{0,1:T(8,128)(2,1)}), bf16[256,32]{0,1:T(8,128)(2,1)}) %reduce-scatter.31.cloned.1.call-update) | async-done | bytes 16400 | tf_op jit(solution)/shard_map/reduce_scatter | solution.py:272
  738.5 58.3 %reduce-scatter.29.cloned.1.call-done = bf16[256,32]{0,1:T(8,128)(2,1)} async-done(((bf16[256,512]{0,1:T(8,128)(2,1)}), bf16[256,32]{0,1:T(8,128)(2,1)}) %reduce-scatter.29.cloned.1.call-update) | async-done | bytes 16400 | tf_op jit(solution)/shard_map/reduce_scatter | solution.py:272
  798.2 99.0 %all-reduce.18.cloned.1.call-done = (bf16[3,512,256]{2,0,1:T(4,128)(2,1)}, bf16[3,512,256]{2,0,1:T(4,128)(2,1)}) async-done(((bf16[3,512,256]{2,0,1:T(4,128)(2,1)}, bf16[3,512,256]{2,0,1:T(4,128)(2,1)}), (bf16[3,512,256]{2,0,1:T(4,128)(2,1)}, bf16[3,512,256]{2,0,1:T(4,128)(2,1)})) %all-reduce.18.cloned.1.call-update) | async-done | bytes 1572880
  898.8 62.9 %all-reduce.20.cloned.1.call-done = (bf16[1024,512]{1,0:T(8,128)(2,1)}, bf16[1024,512]{1,0:T(8,128)(2,1)}) async-done(((bf16[1024,512]{1,0:T(8,128)(2,1)}, bf16[1024,512]{1,0:T(8,128)(2,1)}), (bf16[1024,512]{1,0:T(8,128)(2,1)}, bf16[1024,512]{1,0:T(8,128)(2,1)})) %all-reduce.20.cloned.1.call-update) | async-done | bytes 2097168 | tf_op jit(solution)/shard_map/psum | solution.py:191
  977.4 44.8 %reduce-scatter.45.cloned.1.call-done = bf16[32,2]{1,0:T(8,128)(2,1)} async-done(((bf16[512,2]{1,0:T(8,128)(2,1)}), bf16[32,2]{1,0:T(8,128)(2,1)}) %reduce-scatter.45.cloned.1.call-update) | async-done | bytes 144
  1022.9 57.4 %reduce-scatter.47.cloned.1.call-done = bf16[32,2]{1,0:T(8,128)(2,1)} async-done(((bf16[512,2]{1,0:T(8,128)(2,1)}), bf16[32,2]{1,0:T(8,128)(2,1)}) %reduce-scatter.47.cloned.1.call-update) | async-done | bytes 144
  1081.1 57.4 %reduce-scatter.49.cloned.1.call-done = bf16[32,2]{1,0:T(8,128)(2,1)} async-done(((bf16[512,2]{1,0:T(8,128)(2,1)}), bf16[32,2]{1,0:T(8,128)(2,1)}) %reduce-scatter.49.cloned.1.call-update) | async-done | bytes 144
  1139.3 57.4 %reduce-scatter.51.cloned.1.call-done = bf16[32,2]{1,0:T(8,128)(2,1)} async-done(((bf16[512,2]{1,0:T(8,128)(2,1)}), bf16[32,2]{1,0:T(8,128)(2,1)}) %reduce-scatter.51.cloned.1.call-update) | async-done | bytes 144
  (365 shorter events, 183.1 us)
Async XLA Ops:
  8.0 85.3 %copy-start.2 = (bf16[2,1024,512]{2,1,0:T(8,128)(2,1)S(1)}, bf16[2,1024,512]{2,1,0:T(8,128)(2,1)}, u32[]{:S(2)}) copy-start(bf16[2,1024,512]{2,1,0:T(8,128)(2,1)} %param.13) | copy-start | bytes 6291460
  8.0 65.6 %copy-start.57 = (bf16[3,32,256]{2,1,0:T(8,128)(2,1)S(1)}, bf16[3,32,256]{2,1,0:T(8,128)(2,1)}, u32[]{:S(2)}) copy-start(bf16[3,32,256]{2,1,0:T(8,128)(2,1)} %param.15) | copy-start | bytes 147460
  8.0 255.1 %all-reduce.16.cloned.1.call-start = ((), (), s32[]{:S(2)}) async-start(), calls=%async_computation.28 | async-start | bytes 8388608 | tf_op jit(solution)/shard_map/psum | solution.py:85
  32.4 61.9 %copy-start.58 = (f32[1,512]{1,0:T(1,128)}, f32[1,512]{1,0:T(1,128)S(1)}, u32[]{:S(2)}) copy-start(f32[1,512]{1,0:T(1,128)S(1)} %get-tuple-element.127) | copy-start | bytes 6148
  50.1 44.2 %copy-start.61 = (f32[1,512]{1,0:T(1,128)}, f32[1,512]{1,0:T(1,128)S(1)}, u32[]{:S(2)}) copy-start(f32[1,512]{1,0:T(1,128)S(1)} %get-tuple-element.129) | copy-start | bytes 6148
  52.0 42.7 %copy-start.49 = (f32[1024]{0:T(1024)}, f32[1024]{0:T(1024)S(1)}, u32[]{:S(2)}) copy-start(f32[1024]{0:T(1024)S(1)} %get-tuple-element.154) | copy-start | bytes 12292
  52.0 42.7 %copy-start.51 = (f32[1024]{0:T(1024)}, f32[1024]{0:T(1024)S(1)}, u32[]{:S(2)}) copy-start(f32[1024]{0:T(1024)S(1)} %get-tuple-element.155) | copy-start | bytes 12292
  54.4 41.6 %copy-start.53 = (f32[1024]{0:T(1024)}, f32[1024]{0:T(1024)S(1)}, u32[]{:S(2)}) copy-start(f32[1024]{0:T(1024)S(1)} %add_rsqrt_fusion.3) | copy-start | bytes 12292
  54.5 41.6 %copy-start.55 = (f32[1024]{0:T(1024)}, f32[1024]{0:T(1024)S(1)}, u32[]{:S(2)}) copy-start(f32[1024]{0:T(1024)S(1)} %add_rsqrt_fusion.1) | copy-start | bytes 12292
  94.8 36.5 %copy-start.18 = (bf16[1024,256]{0,1:T(8,128)(2,1)}, bf16[1024,256]{0,1:T(8,128)(2,1)S(1)}, u32[]{:S(2)}) copy-start(bf16[1024,256]{0,1:T(8,128)(2,1)S(1)} %convolution_convert_fusion.17) | copy-start | bytes 1572868
  99.2 26.3 %copy-start.24 = (bf16[1024,256]{0,1:T(8,128)(2,1)}, bf16[1024,256]{0,1:T(8,128)(2,1)S(1)}, u32[]{:S(2)}) copy-start(bf16[1024,256]{0,1:T(8,128)(2,1)S(1)} %fusion.109) | copy-start | bytes 1572868
  99.7 25.8 %copy-start.16 = (bf16[1024,256]{0,1:T(8,128)(2,1)}, bf16[1024,256]{0,1:T(8,128)(2,1)S(1)}, u32[]{:S(2)}) copy-start(bf16[1024,256]{0,1:T(8,128)(2,1)S(1)} %convolution_convert_fusion.15) | copy-start | bytes 1572868
  119.8 338.5 %copy-start.14 = (bf16[256,512]{0,1:T(8,128)(2,1)}, bf16[256,512]{0,1:T(8,128)(2,1)S(1)}, u32[]{:S(2)}) copy-start(bf16[256,512]{0,1:T(8,128)(2,1)S(1)} %all_gather.52) | copy-start | bytes 786436
  157.8 110.2 %all-gather.11.cloned.1.call-start = ((), (), s32[]{:S(2)}) async-start(), calls=%async_computation.12 | async-start | bytes 1114112 | tf_op jit(solution)/shard_map/all_gather | solution.py:248
  158.4 115.0 %all-gather.13.cloned.1.call-start = ((), (), s32[]{:S(2)}) async-start(), calls=%async_computation.13 | async-start | bytes 1114112 | tf_op jit(solution)/shard_map/all_gather | solution.py:249
  159.0 216.1 %all-reduce.22.cloned.1.call-start = ((), (), s32[]{:S(2)}) async-start(), calls=%async_computation.31 | async-start | bytes 4194304 | tf_op jit(solution)/shard_map/psum | solution.py:147
  311.9 97.8 %all-gather.17.cloned.1.call-start = ((), (), s32[]{:S(2)}) async-start(), calls=%async_computation.21 | async-start | bytes 3145728 | tf_op jit(solution)/shard_map/all_gather | solution.py:93
  316.2 128.1 %all-gather.15.cloned.1.call-start = ((), (), s32[]{:S(2)}) async-start(), calls=%async_computation.20 | async-start | bytes 3145728 | tf_op jit(solution)/shard_map/all_gather | solution.py:93
  320.9 258.5 %reduce-scatter.35.cloned.1.call-start = ((), (), s32[]{:S(2)}) async-start(), calls=%async_computation.17 | async-start | bytes 1114112 | tf_op jit(solution)/shard_map/reduce_scatter | solution.py:275
  325.8 253.6 %reduce-scatter.33.cloned.1.call-start = ((), (), s32[]{:S(2)}) async-start(), calls=%async_computation.16 | async-start | bytes 1114112 | tf_op jit(solution)/shard_map/reduce_scatter | solution.py:275
  330.0 251.0 %reduce-scatter.39.cloned.1.call-start = ((), (), s32[]{:S(2)}) async-start(), calls=%async_computation.19 | async-start | bytes 1114112 | tf_op jit(solution)/shard_map/reduce_scatter | solution.py:278
  334.4 246.6 %reduce-scatter.37.cloned.1.call-start = ((), (), s32[]{:S(2)}) async-start(), calls=%async_computation.18 | async-start | bytes 1114112 | tf_op jit(solution)/shard_map/reduce_scatter | solution.py:278
  338.7 312.9 %reduce-scatter.41.cloned.1.call-start = ((), (), s32[]{:S(2)}) async-start(), calls=%async_computation.22 | async-start | bytes 139264
  544.3 136.0 %reduce-scatter.43.cloned.1.call-start = ((), (), s32[]{:S(2)}) async-start(), calls=%async_computation.23 | async-start | bytes 139264
  545.2 193.3 %reduce-scatter.31.cloned.1.call-start = ((), (), s32[]{:S(2)}) async-start(), calls=%async_computation.15 | async-start | bytes 278528 | tf_op jit(solution)/shard_map/reduce_scatter | solution.py:272
  552.4 244.4 %reduce-scatter.29.cloned.1.call-start = ((), (), s32[]{:S(2)}) async-start(), calls=%async_computation.14 | async-start | bytes 278528 | tf_op jit(solution)/shard_map/reduce_scatter | solution.py:272
  565.7 331.5 %all-reduce.18.cloned.1.call-start = ((), (), s32[]{:S(2)}) async-start(), calls=%async_computation.29 | async-start | bytes 4194304
  571.7 389.9 %all-reduce.20.cloned.1.call-start = ((), (), s32[]{:S(2)}) async-start(), calls=%async_computation.30 | async-start | bytes 4194304 | tf_op jit(solution)/shard_map/psum | solution.py:191
  577.3 444.8 %reduce-scatter.45.cloned.1.call-start = ((), (), s32[]{:S(2)}) async-start(), calls=%async_computation.24 | async-start | bytes 139264
  966.4 113.9 %reduce-scatter.47.cloned.1.call-start = ((), (), s32[]{:S(2)}) async-start(), calls=%async_computation.25 | async-start | bytes 139264
  968.8 169.7 %reduce-scatter.49.cloned.1.call-start = ((), (), s32[]{:S(2)}) async-start(), calls=%async_computation.26 | async-start | bytes 139264
  969.9 226.7 %reduce-scatter.51.cloned.1.call-start = ((), (), s32[]{:S(2)}) async-start(), calls=%async_computation.27 | async-start | bytes 139264
  (74 other events, 538.7 us)
Sparse Core Ops, SparseCore 0:
  157.9 105.1 all-reduce.15
  312.1 62.9 all-reduce.21
  376.6 33.0 all-gather.16
  411.2 33.0 all-gather.14
Sparse Core Ops, SparseCore 1:
  160.4 35.0 all-gather.10
  197.5 36.8 all-gather.12
  325.9 57.3 reduce-scatter.34
  386.9 56.6 reduce-scatter.32
  447.3 56.6 reduce-scatter.38
  507.6 56.6 reduce-scatter.36
  567.6 54.6 reduce-scatter.40
  625.6 54.6 reduce-scatter.42
  683.6 54.8 reduce-scatter.30
  742.0 54.7 reduce-scatter.28
  800.3 96.9 all-reduce.17
  899.6 62.0 all-reduce.19
  966.5 55.6 reduce-scatter.44
  1025.7 54.6 reduce-scatter.46
  1083.8 54.6 reduce-scatter.48
  1142.0 54.6 reduce-scatter.50
